TPU v7x, 128 devices: a whole 4x4x4 slice. The times are simulated.
128 devices in a mesh: tab: 32 (over x, y, core), rep: 4 (over z).
Axes of the slice: x: 4, y: 4, z: 4, core: 2. Of those that a mesh axis runs over, the one named last changes fastest.
Arguments:
- pooled: bfloat16 [64, 16384, 128], P('tab', 'rep'), may hold values from -6 to 6
- widths: int32 [64], replicated, may hold values from 16 to 128, as said below
- placement: int32 [64], replicated, may hold values from 0 to 63, each once
- route: int32 [4, 4096], P('rep'), may hold values from 0 to 4095, each once within a row
- labels: int32 [4, 4096], P('rep'), may hold values 0 or 1
- proj: bfloat16 [64, 128, 32], replicated, may hold values from -0.5 to 0.5
- senet_in: float32 [64, 32], replicated, may hold values from -6 to 6
- senet_out: float32 [32, 64], replicated, may hold values from -1 to 1
- bilinear: float32 [32, 32], replicated, may hold values from -1 to 1
- w_first: bfloat16 [4096, 256], replicated, may hold values from -0.09375 to 0.09375
- w_second: bfloat16 [256, 256], replicated, may hold values from -0.75 to 0.75
- w_last: bfloat16 [256], replicated, may hold values from -0.375 to 0.375
Outputs:
- scores: float32 [4, 4096], P('rep', 'tab')
- d_pooled: bfloat16 [64, 16384, 128], P('tab', 'rep')
- d_proj: float32 [64, 128, 32], P('tab')
- d_senet_in: float32 [64, 32], replicated
- d_senet_out: float32 [32, 64], replicated
- d_bilinear: float32 [32, 32], replicated
- d_first: float32 [4096, 256], P('tab')
- d_second: float32 [256, 256], replicated
- d_last: float32 [256], replicated
Inputs may be any that keep to these rules, and one draw needn't show every extreme that they name: `widths`: each field's width is 128, 64, 32 or 16. `placement`: a permutation of the fields. `route`: each row is a permutation of 0 to 4095.
All inputs are finite; a program needn't handle non-finite values. No bound on the sum of `labels` on one device may be relied on, other than what follows from the above.
Results may differ from a plain program's by a relative error of at most 0.017.
Values may be sent and summed in bfloat16 or wider, within the bound.
A program may use at most 64 MiB of HBM per device.

v0:
```python
import jax
import jax.numpy as jnp
from jax import lax
from jax.sharding import PartitionSpec as P


def sent_to_all(value, axis):
    peers = lax.axis_size(axis)
    return lax.all_to_all(
        jnp.broadcast_to(value[None], (peers, *value.shape)), axis, 0, 0, tiled=True
    )


def of_everyone(value, axis):
    everything = sent_to_all(value, axis)
    return jnp.sum(everything.astype(jnp.float32), axis=0)


def laid_out(pieces, dim):
    lengths = list(pieces.shape[1:])
    lengths[dim] *= pieces.shape[0]
    return jnp.moveaxis(pieces, 0, dim).reshape(lengths)


def collect(value, axis, dim):
    pieces = sent_to_all(value, axis)
    return laid_out(pieces, dim)


def silu_slope(pre_act):
    logistic = jax.nn.sigmoid(pre_act)
    return logistic * (1.0 + pre_act * (1.0 - logistic))


def bilinear_forward(fields_in, bilinear, factor):
    product = jnp.einsum("fnc,cd->fnd", fields_in, bilinear)
    others = jnp.sum(fields_in, axis=0, keepdims=True) - fields_in
    return (product * others * factor, product, others)


def bilinear_backward(fields_in, product, others, upstream, bilinear, factor):
    d_product = upstream * others * factor
    d_others = upstream * product * factor
    d_fields = jnp.einsum("fnd,cd->fnc", d_product, bilinear)
    d_fields = d_fields + jnp.sum(d_others, axis=0, keepdims=True) - d_others
    d_weight = jnp.einsum("fnc,fnd->cd", fields_in, d_product)
    return (d_fields, d_weight)


def owner_pass(embeds, targets, senet_in, senet_out, bilinear, w_first, w_second, w_last):
    count = embeds.shape[0]
    width = embeds.shape[2]
    hidden = w_second.shape[0]
    factor = count ** (-0.5)
    first = w_first.reshape(2, count, width, hidden)
    dense = embeds.astype(jnp.float32)
    squeeze = jnp.mean(dense, axis=2)
    pre_one = jnp.einsum("fn,fr->rn", squeeze, senet_in)
    act_one = jax.nn.silu(pre_one)
    pre_two = jnp.einsum("rn,rf->fn", act_one, senet_out)
    weights = jax.nn.sigmoid(pre_two)
    scaled = weights[:, :, None] * dense
    plain_out, plain_prod, plain_rest = bilinear_forward(dense, bilinear, factor)
    scaled_out, scaled_prod, scaled_rest = bilinear_forward(scaled, bilinear, factor)
    joined = jnp.stack([plain_out, scaled_out]).astype(jnp.bfloat16)
    pre_hidden = jnp.einsum("kfnc,kfch->nh", joined, first, preferred_element_type=jnp.float32)
    hidden_one = jax.nn.silu(pre_hidden).astype(jnp.bfloat16)
    pre_second = jnp.dot(hidden_one, w_second, preferred_element_type=jnp.float32)
    hidden_two = jax.nn.silu(pre_second).astype(jnp.bfloat16)
    logits = jnp.dot(hidden_two, w_last, preferred_element_type=jnp.float32)
    grad_logit = jax.nn.sigmoid(logits) - targets
    d_last = jnp.dot(grad_logit, hidden_two.astype(jnp.float32))
    last_wide = w_last.astype(jnp.float32)
    d_pre_two = (grad_logit[:, None] * last_wide[None, :] * silu_slope(pre_second)).astype(
        jnp.bfloat16
    )
    d_second = jnp.dot(hidden_one.T, d_pre_two, preferred_element_type=jnp.float32)
    back_two = jnp.dot(d_pre_two, w_second.T, preferred_element_type=jnp.float32)
    d_pre_one = (back_two * silu_slope(pre_hidden)).astype(jnp.bfloat16)
    d_first = jnp.einsum(
        "kfnc,nh->kfch", joined, d_pre_one, preferred_element_type=jnp.float32
    ).reshape(-1, hidden)
    d_joined = jnp.einsum("nh,kfch->kfnc", d_pre_one, first, preferred_element_type=jnp.float32)
    d_plain, d_bil_plain = bilinear_backward(
        dense, plain_prod, plain_rest, d_joined[0], bilinear, factor
    )
    d_scaled, d_bil_scaled = bilinear_backward(
        scaled, scaled_prod, scaled_rest, d_joined[1], bilinear, factor
    )
    d_weights = jnp.sum(d_scaled * dense, axis=2)
    d_pre_w = d_weights * weights * (1.0 - weights)
    d_senet_out = jnp.einsum("rn,fn->rf", act_one, d_pre_w)
    d_act = jnp.einsum("fn,rf->rn", d_pre_w, senet_out) * silu_slope(pre_one)
    d_senet_in = jnp.einsum("fn,rn->fr", squeeze, d_act)
    d_squeeze = jnp.einsum("rn,fr->fn", d_act, senet_in)
    d_embeds = d_plain + weights[:, :, None] * d_scaled + d_squeeze[:, :, None] / width
    small = (d_senet_in, d_senet_out, d_bil_plain + d_bil_scaled, d_second, d_last)
    return (logits, d_embeds.astype(jnp.bfloat16), small, d_first, joined, d_pre_one)


def shards(
    pooled,
    widths,
    placement,
    route,
    labels,
    proj,
    senet_in,
    senet_out,
    bilinear,
    w_first,
    w_second,
    w_last,
):
    tab_count = lax.axis_size("tab")
    tab_index = lax.axis_index("tab")
    local_count = pooled.shape[0]
    rep_rows = pooled.shape[1]
    padded = pooled.shape[2]
    field_count = placement.shape[0]
    owner_rows = rep_rows // tab_count
    field_ids = jnp.arange(field_count, dtype=jnp.int32)
    matches = placement[:, None] == field_ids[None, :]
    slot_width = jnp.sum(jnp.where(matches, widths[None, :], 0), axis=1)
    slot_mask = (jnp.arange(padded, dtype=jnp.int32)[None, :] < slot_width[:, None]).astype(
        jnp.bfloat16
    )
    inverse = jnp.zeros_like(placement).at[placement].set(field_ids)
    targets = lax.dynamic_slice_in_dim(labels[0], tab_index * owner_rows, owner_rows).astype(
        jnp.float32
    )
    first_slot = tab_index * local_count
    local_fields = lax.dynamic_slice_in_dim(placement, first_slot, local_count)
    local_mask = lax.dynamic_slice_in_dim(slot_mask, first_slot, local_count, 0)
    local_proj = jnp.take(proj, local_fields, axis=0)
    masked = pooled * local_mask[:, None, :]
    embed_local = jnp.einsum(
        "fnc,fcd->fnd", masked, local_proj, preferred_element_type=jnp.float32
    ).astype(jnp.bfloat16)
    embed_slot = lax.all_to_all(embed_local, "tab", split_axis=1, concat_axis=0, tiled=True)
    logits, d_embeds, small, d_first_part, joined, d_pre_one = owner_pass(
        embed_slot[inverse], targets, senet_in, senet_out, bilinear, w_first, w_second, w_last
    )
    d_slot = d_embeds[placement]
    d_local = lax.all_to_all(d_slot, "tab", split_axis=0, concat_axis=1, tiled=True)
    back = jnp.einsum("fnd,fcd->fnc", d_local, local_proj, preferred_element_type=jnp.float32)
    back = (back * local_mask[:, None, :]).astype(jnp.bfloat16)
    d_proj_part = jnp.einsum("fnc,fnd->fcd", masked, d_local, preferred_element_type=jnp.float32)
    d_proj = of_everyone(d_proj_part.astype(jnp.bfloat16), "rep").astype(jnp.float32)
    first_tab = lax.psum_scatter(
        d_first_part.astype(jnp.bfloat16), "tab", scatter_dimension=0, tiled=True
    )
    d_first = of_everyone(first_tab, "rep").astype(jnp.float32)
    part_in, part_out, part_bil, part_second, part_last = small
    d_senet_in, d_senet_out, d_bilinear, d_second, d_last = lax.psum(
        (part_in, part_out, part_bil, part_second, part_last), ("tab", "rep")
    )
    all_logits = collect(logits, "tab", 0)
    wanted = lax.dynamic_slice_in_dim(route[0], tab_index * owner_rows, owner_rows)
    scores = jnp.take(all_logits, wanted)[None, :]
    return (scores, back, d_proj, d_senet_in, d_senet_out, d_bilinear, d_first, d_second, d_last)


def solution(mesh):
    placed = (
        P("tab", "rep", None),
        P(),
        P(),
        P("rep", None),
        P("rep", None),
        P(),
        P(),
        P(),
        P(),
        P(),
        P(),
        P(),
    )
    return jax.shard_map(
        shards,
        mesh=mesh,
        in_specs=placed,
        out_specs=(
            P("rep", "tab"),
            P("tab", "rep", None),
            P("tab", None, None),
            P(),
            P(),
            P(),
            P("tab", None),
            P(),
            P(),
        ),
        check_vma=False,
    )
```

profile of v0, /device:TPU:1, one launch (start us, length us, event | category | flops | bytes accessed | tf_op | source)
XLA Modules:
  0.0 225.5 jit_solution(7572727441180644628)
XLA Ops:
  8.0 1.0 select_reduce_fusion
  9.0 0.7 compare_and_fusion
  9.8 0.1 dynamic-slice.2
  9.8 0.1 fusion.98
  9.9 1.6 gather_fusion
  11.5 2.4 %convolution_convert_fusion = bf16[2,4096,32]{1,2,0:T(8,128)(2,1)S(1)} fusion(bf16[2,4096,128]{2,1,0:T(8,128)(2,1)} %param.12, bf16[2,128]{1,0:T(2,128)(2,1)S(1)} %get-tuple-element.22, bf16[2,128,32]{1,2,0:T(8,128)(2,1)S(1)} %gather_fusion, pred[2]{0:T(512)(128)(4,1)S(1)} %get-tuple-element.17), kind=kOutput, calls=%fused_computation.7 | convolution fusion | flops 68427776 | bytes 2638338 | tf_op jit(solution)/shard_map/fnc,fcd->fnd/dot_general | solution.py:137
  14.0 3.8 %copy.56 = bf16[2,4096,32]{2,0,1:T(2,128)(2,1)} copy(bf16[2,4096,32]{1,2,0:T(8,128)(2,1)S(1)} %convolution_convert_fusion) | data formatting | bytes 1048576 | tf_op jit(solution)/shard_map/convert_element_type | solution.py:139
  17.8 5.9 %reshape.152 = bf16[32,2,4096]{2,1,0:T(2,128)(2,1)} reshape(bf16[4096,2,32]{2,1,0:T(2,128)(2,1)} %bitcast.166) | data formatting | bytes 1048576
  23.7 8.6 %all-to-all-start = ((bf16[32,2,4096]{2,1,0:T(2,128)(2,1)}), bf16[32,2,4096]{2,1,0:T(2,128)(2,1)S(1)}, u32[]{:S(2)}, u32[]{:S(2)}) async-start(bf16[32,2,4096]{2,1,0:T(2,128)(2,1)} %reshape.152), calls=%async_computation | async-start | bytes 1048576 | tf_op jit(solution)/shard_map/all_to_all | solution.py:140
  32.3 0.0 reduce-scatter.2.cloned.1.call-start
  32.4 0.8 scatter_custom_fusion
  33.2 10.7 %all-to-all-done = bf16[32,2,4096]{2,1,0:T(2,128)(2,1)S(1)} async-done(((bf16[32,2,4096]{2,1,0:T(2,128)(2,1)}), bf16[32,2,4096]{2,1,0:T(2,128)(2,1)S(1)}, u32[]{:S(2)}, u32[]{:S(2)}) %all-to-all-start) | async-done | bytes 524320 | tf_op jit(solution)/shard_map/all_to_all | solution.py:140
  43.9 2.0 reshape.153
  45.8 4.7 %copy.73 = bf16[2,32,128,32]{2,3,0,1:T(8,128)(2,1)S(1)} copy(bf16[2,32,128,32]{3,0,2,1:T(2,128)(2,1)} %bitcast.167) | data formatting | bytes 1048576 | tf_op jit(solution)/shard_map/all_to_all | solution.py:140
  50.5 0.7 gather_fusion.1
  51.2 0.1 convert_reduce_fusion
  51.4 0.1 convolution_bitcast_fusion.3
  51.5 0.2 fusion.28
  51.7 0.2 convert_reduce_fusion.1
  51.9 0.3 fusion.9
  52.2 0.3 fusion.106
  52.6 0.4 fusion.49
  53.0 0.2 copy-done.4
  53.2 0.5 fusion.19
  53.8 0.4 copy-done.9
  54.1 0.2 multiply_convert_fusion.1
  54.3 0.8 divide_subtract_fusion
  55.1 0.2 fusion.23
  55.4 2.0 convolution_convert_fusion.1
  57.4 0.7 fusion.82
  58.1 0.6 broadcast_in_dim.45
  58.7 3.6 %all-to-all-start.1 = ((f32[32,1,128]{2,1,0:T(1,128)}), f32[32,1,128]{2,1,0:T(1,128)S(1)}, u32[]{:S(2)}, u32[]{:S(2)}) async-start(f32[32,1,128]{2,1,0:T(1,128)} %broadcast_in_dim.45), calls=%async_computation.1 | async-start | bytes 32768 | tf_op jit(solution)/shard_map/all_to_all | solution.py:9
  62.4 0.0 all-reduce.3.cloned.1.call-start
  62.4 0.7 convolution_bitcast_fusion
  63.2 0.3 convolution_bitcast_fusion.1
  63.5 1.7 copy-done.3
  65.1 0.3 copy-done.5
  65.4 0.5 fusion.66
  66.0 1.5 fusion.41
  67.5 0.1 fusion.33
  67.6 0.2 fusion.24
  67.8 0.1 fusion.111
  68.0 0.1 fusion.79
  68.1 1.0 fusion.99
  69.1 2.7 %fusion.14 = bf16[64,128,32]{1,2,0:T(8,128)(2,1)S(1)} fusion(f32[64,128,32]{1,2,0:T(8,128)} %get-tuple-element.28, bf16[64,128,32]{1,2,0:T(8,128)(2,1)S(1)} %gather_fusion.1, f32[2,64,128,32]{2,3,1,0:T(8,128)} %copy-done.1, f32[64,128]{1,0:T(8,128)S(1)} %fusion.24, f32[128,32]{0,1:T(8,128)S(1)} %get-tuple-element.9, f32[64,128]{1,0:T(8,128)S(1)} %fusion.28, ...), kind=kOutput, calls=%fused_computation.30 | convolution fusion | flops 19922944 | bytes 5345280 | tf_op jit(solution)/shard_map/fnd,cd->fnc/dot_general | solution.py:44
  71.8 1.4 gather_fusion.3
  73.2 7.4 %all-to-all-start.2 = ((bf16[64,128,32]{1,2,0:T(8,128)(2,1)}), bf16[64,128,32]{1,2,0:T(8,128)(2,1)S(1)}, u32[]{:S(2)}, u32[]{:S(2)}) async-start(bf16[64,128,32]{1,2,0:T(8,128)(2,1)} %gather_fusion.3), calls=%async_computation.2 | async-start | bytes 1048576 | tf_op jit(solution)/shard_map/all_to_all | solution.py:145
  80.6 0.1 fusion.68
  80.7 1.6 fusion.34
  82.4 68.8 %all-reduce = (f32[64,32]{0,1:T(8,128)}, f32[32,64]{1,0:T(8,128)}, f32[32,32]{1,0:T(8,128)}, f32[256]{0:T(256)}) all-reduce(f32[64,32]{0,1:T(8,128)S(1)} %fusion.68, f32[32,64]{1,0:T(8,128)S(1)} %fusion.79, f32[32,32]{1,0:T(8,128)S(1)} %fusion.34, f32[256]{0:T(256)S(1)} %bitcast.171), channel_id=1, replica_groups=mesh['tab'=32,'rep'=4] {'tab','rep'}, use_global_device_ids=true, to_apply=%region_9.10 | all-reduce | flops 5376 | bytes 43008 | tf_op jit(solution)/shard_map/psum | solution.py:155
  151.2 1.1 gather_fusion.2
  152.4 2.2 fusion.29
  154.5 0.6 broadcast_in_dim.49
  155.2 3.3 %all-to-all-start.3 = ((bf16[4,2,128,32]{2,3,1,0:T(8,128)(2,1)}), bf16[4,2,128,32]{2,3,1,0:T(8,128)(2,1)S(1)}, u32[]{:S(2)}, u32[]{:S(2)}) async-start(bf16[4,2,128,32]{2,3,1,0:T(8,128)(2,1)} %broadcast_in_dim.49), calls=%async_computation.3 | async-start | bytes 131072 | tf_op jit(solution)/shard_map/all_to_all | solution.py:9
  158.5 1.2 and_select_fusion
  159.7 3.3 %all-to-all-done.3 = bf16[4,2,128,32]{2,3,1,0:T(8,128)(2,1)S(1)} async-done(((bf16[4,2,128,32]{2,3,1,0:T(8,128)(2,1)}), bf16[4,2,128,32]{2,3,1,0:T(8,128)(2,1)S(1)}, u32[]{:S(2)}, u32[]{:S(2)}) %all-to-all-start.3) | async-done | bytes 65568 | tf_op jit(solution)/shard_map/all_to_all | solution.py:9
  162.9 1.6 broadcast_in_dim.82
  164.5 3.4 %all-to-all-start.4 = ((bf16[4,128,256]{2,1,0:T(8,128)(2,1)}), bf16[4,128,256]{2,1,0:T(8,128)(2,1)S(1)}, u32[]{:S(2)}, u32[]{:S(2)}) async-start(bf16[4,128,256]{2,1,0:T(8,128)(2,1)} %broadcast_in_dim.82), calls=%async_computation.5 | async-start | bytes 524288 | tf_op jit(solution)/shard_map/all_to_all | solution.py:9
  167.9 2.3 %fusion = bf16[2,4096,128]{2,1,0:T(8,128)(2,1)} fusion(f32[2,128]{1,0:T(2,128)S(1)} %get-tuple-element.21, bf16[32,2,4,8,128]{4,3,2,1,0:T(8,128)(2,1)S(1)} %bitcast.170, bf16[2,128,32]{1,2,0:T(8,128)(2,1)S(1)} %gather_fusion, pred[2]{0:T(512)(128)(4,1)S(1)} %get-tuple-element.17), kind=kOutput, calls=%fused_computation.6 | convolution fusion | flops 69214208 | bytes 2638850 | tf_op jit(solution)/shard_map/fnd,fcd->fnc/dot_general | solution.py:146
  170.1 0.6 convert_reduce_fusion.3
  170.8 2.6 %all-to-all-done.4 = bf16[4,128,256]{2,1,0:T(8,128)(2,1)S(1)} async-done(((bf16[4,128,256]{2,1,0:T(8,128)(2,1)}), bf16[4,128,256]{2,1,0:T(8,128)(2,1)S(1)}, u32[]{:S(2)}, u32[]{:S(2)}) %all-to-all-start.4) | async-done | bytes 262176 | tf_op jit(solution)/shard_map/all_to_all | solution.py:9
  173.4 0.7 convert_reduce_fusion.2
  174.1 42.3 %all-reduce.3.cloned.1.call-done = f32[256,256]{1,0:T(8,128)} async-done(((f32[256,256]{1,0:T(8,128)}), f32[256,256]{1,0:T(8,128)}) %all-reduce.3.cloned.1.call-update) | async-done | bytes 262160 | tf_op jit(solution)/shard_map/psum | solution.py:155
  216.3 1.7 copy.92
  (34 shorter events, 0.1 us)
Async XLA Ops:
  8.0 45.2 %copy-start = (bf16[4096,256]{1,0:T(8,128)(2,1)S(1)}, bf16[4096,256]{1,0:T(8,128)(2,1)}, u32[]{:S(2)}) copy-start(bf16[4096,256]{1,0:T(8,128)(2,1)} %param.21) | copy-start | bytes 6291460
  17.8 14.5 %copy-start.11 = (bf16[256]{0:T(256)(128)(2,1)S(1)}, bf16[256]{0:T(256)(128)(2,1)}, u32[]{:S(2)}) copy-start(bf16[256]{0:T(256)(128)(2,1)} %param.23) | copy-start | bytes 1540
  17.8 14.5 %copy-start.8 = (s32[64]{0:T(128)S(1)}, s32[64]{0:T(128)}, u32[]{:S(2)}) copy-start(s32[64]{0:T(128)} %param.14) | copy-start | bytes 772
  23.7 20.2 %all-to-all-start = ((bf16[32,2,4096]{2,1,0:T(2,128)(2,1)}), bf16[32,2,4096]{2,1,0:T(2,128)(2,1)S(1)}, u32[]{:S(2)}, u32[]{:S(2)}) async-start(bf16[32,2,4096]{2,1,0:T(2,128)(2,1)} %reshape.152), calls=%async_computation | async-start | bytes 1048576 | tf_op jit(solution)/shard_map/all_to_all | solution.py:140
  32.3 130.7 %reduce-scatter.2.cloned.1.call-start = ((), (), s32[]{:S(2)}) async-start(), calls=%async_computation.6 | async-start | bytes 2162688 | tf_op jit(solution)/shard_map/reduce_scatter | solution.py:150
  50.5 0.8 copy-start.7
  50.5 1.0 copy-start.10
  50.5 1.3 copy-start.6
  52.2 1.0 copy-start.4
  52.6 1.2 copy-start.2
  53.2 0.9 copy-start.9
  58.7 14.5 %all-to-all-start.1 = ((f32[32,1,128]{2,1,0:T(1,128)}), f32[32,1,128]{2,1,0:T(1,128)S(1)}, u32[]{:S(2)}, u32[]{:S(2)}) async-start(f32[32,1,128]{2,1,0:T(1,128)} %broadcast_in_dim.45), calls=%async_computation.1 | async-start | bytes 32768 | tf_op jit(solution)/shard_map/all_to_all | solution.py:9
  62.4 154.0 %all-reduce.3.cloned.1.call-start = ((), (), s32[]{:S(2)}) async-start(), calls=%async_computation.7 | async-start | bytes 524288 | tf_op jit(solution)/shard_map/psum | solution.py:155
  63.1 2.8 %copy-start.1 = (f32[2,64,128,32]{2,3,1,0:T(8,128)}, f32[2,64,128,32]{2,3,1,0:T(8,128)S(1)}, u32[]{:S(2)}) copy-start(f32[2,64,128,32]{2,3,1,0:T(8,128)S(1)} %convolution_bitcast_fusion) | copy-start | bytes 6291460
  63.1 2.0 copy-start.3
  63.1 2.3 %copy-start.5 = (f32[64,128,32]{1,2,0:T(8,128)S(1)}, f32[64,128,32]{1,2,0:T(8,128)}, u32[]{:S(2)}) copy-start(f32[64,128,32]{1,2,0:T(8,128)} %copy-done.4) | copy-start | bytes 3145732
  73.2 79.1 %all-to-all-start.2 = ((bf16[64,128,32]{1,2,0:T(8,128)(2,1)}), bf16[64,128,32]{1,2,0:T(8,128)(2,1)S(1)}, u32[]{:S(2)}, u32[]{:S(2)}) async-start(bf16[64,128,32]{1,2,0:T(8,128)(2,1)} %gather_fusion.3), calls=%async_computation.2 | async-start | bytes 1048576 | tf_op jit(solution)/shard_map/all_to_all | solution.py:145
  155.2 7.7 %all-to-all-start.3 = ((bf16[4,2,128,32]{2,3,1,0:T(8,128)(2,1)}), bf16[4,2,128,32]{2,3,1,0:T(8,128)(2,1)S(1)}, u32[]{:S(2)}, u32[]{:S(2)}) async-start(bf16[4,2,128,32]{2,3,1,0:T(8,128)(2,1)} %broadcast_in_dim.49), calls=%async_computation.3 | async-start | bytes 131072 | tf_op jit(solution)/shard_map/all_to_all | solution.py:9
  164.5 8.9 %all-to-all-start.4 = ((bf16[4,128,256]{2,1,0:T(8,128)(2,1)}), bf16[4,128,256]{2,1,0:T(8,128)(2,1)S(1)}, u32[]{:S(2)}, u32[]{:S(2)}) async-start(bf16[4,128,256]{2,1,0:T(8,128)(2,1)} %broadcast_in_dim.82), calls=%async_computation.5 | async-start | bytes 524288 | tf_op jit(solution)/shard_map/all_to_all | solution.py:9
Sparse Core Ops, SparseCore 0:
  57.6 75.3 reduce-scatter.1
Sparse Core Ops, SparseCore 1:
  69.2 147.1 all-reduce.2
where the time goes:
time: 226 us; the launch traced here: 225 us
  blocking collectives  68.8 us (30%)
  waiting for transfers between devices  58.9 us (26%)
  local copies, waits for them, and re-layouts  29.1 us (13%)
  starting transfers between devices  26.4 us (12%)
  matrix products  20.3 us (9%)
  between operations  15.8 us (7%)
  other arithmetic  6.22 us (3%)
    psum x1, blocking collectives, shards(): lax.psum((part_in, part_out, part_bil, part_second, part_last), ('tab', '...  68.8 us
    psum x1, waiting for transfers between devices, shards(): lax.psum((part_in, part_out, part_bil, part_second, part_last), ('tab', '...  42.3 us
    unnamed x28, local copies, waits for them, and re-layouts  12.1 us
    all_to_all x1, waiting for transfers between devices, shards(): lax.all_to_all(embed_local, 'tab', split_axis=1, concat_axis=0, tiled=True)  10.7 us
    all_to_all x3, starting transfers between devices, sent_to_all(): lax.all_to_all(jnp.broadcast_to(value[None], (peers, *value.shape)), axis...  10.3 us
    all_to_all x1, starting transfers between devices, shards(): lax.all_to_all(embed_local, 'tab', split_axis=1, concat_axis=0, tiled=True)  8.58 us
    all_to_all x1, starting transfers between devices, shards(): lax.all_to_all(d_slot, 'tab', split_axis=0, concat_axis=1, tiled=True)  7.39 us
    all_to_all x3, waiting for transfers between devices, sent_to_all(): lax.all_to_all(jnp.broadcast_to(value[None], (peers, *value.shape)), axis...  5.88 us
  transfers between devices with their start and end apart: 7, of which 4 were waited for; matrix products, arithmetic and copies ran while one was open for 10% of the time, Pallas kernels for 0%

commit v1 on v0

--- a/solution.py
+++ b/solution.py
@@ -112,6 +112,14 @@
     w_second,
     w_last,
 ):
+
+    def track_weights_by_axis(content):
+        axis_id = "tab"
+        which_axis = "rep"
+        for pp in (which_axis, axis_id):
+            content = jax.lax.psum(content, axis_name=pp)
+        return content
+
     tab_count = lax.axis_size("tab")
     tab_index = lax.axis_index("tab")
     local_count = pooled.shape[0]
@@ -152,8 +160,8 @@
     )
     d_first = of_everyone(first_tab, "rep").astype(jnp.float32)
     part_in, part_out, part_bil, part_second, part_last = small
-    d_senet_in, d_senet_out, d_bilinear, d_second, d_last = lax.psum(
-        (part_in, part_out, part_bil, part_second, part_last), ("tab", "rep")
+    d_senet_in, d_senet_out, d_bilinear, d_second, d_last = track_weights_by_axis(
+        (part_in, part_out, part_bil, part_second, part_last)
     )
     all_logits = collect(logits, "tab", 0)
     wanted = lax.dynamic_slice_in_dim(route[0], tab_index * owner_rows, owner_rows)

time: 226 us -> 346 us (1.53)
  blocking collectives: 68.8 us -> 139 us
  waiting for transfers between devices: 58.9 us -> 108 us
    psum x1 -> x2, blocking collectives: 68.8 us -> 139 us  [track_weights_by_axis(): content = jax.lax.psum(content, axis_name=pp)]
    psum x1 -> x2, waiting for transfers between devices: 42.3 us -> 91.6 us  [track_weights_by_axis(): content = jax.lax.psum(content, axis_name=pp)]
    unnamed x28 -> x32, local copies, waits for them, and re-layouts: 12.1 us -> 10.8 us
  transfers between devices with their start and end apart: 7 -> 8, of which waited for: 4 -> 5; matrix products, arithmetic and copies ran while one was open for 10% -> 7% of each run, Pallas kernels for 0% -> 0%
where the time goes in v1:
time: 346 us; the launch traced here: 345 us
  blocking collectives  139 us (40%)
  waiting for transfers between devices  108 us (31%)
  local copies, waits for them, and re-layouts  27.8 us (8%)
  starting transfers between devices  25.9 us (7%)
  matrix products  19.6 us (6%)
  between operations  15.9 us (5%)
  other arithmetic  8.55 us (2%)
    psum x2, blocking collectives, track_weights_by_axis(): content = jax.lax.psum(content, axis_name=pp)  139 us
    psum x2, waiting for transfers between devices, track_weights_by_axis(): content = jax.lax.psum(content, axis_name=pp)  91.6 us
    unnamed x32, local copies, waits for them, and re-layouts  10.8 us
    all_to_all x3, starting transfers between devices, sent_to_all(): lax.all_to_all(jnp.broadcast_to(value[None], (peers, *value.shape)), axis...  10.3 us
    all_to_all x1, waiting for transfers between devices, shards(): lax.all_to_all(embed_local, 'tab', split_axis=1, concat_axis=0, tiled=True)  9.99 us
    all_to_all x1, starting transfers between devices, shards(): lax.all_to_all(embed_local, 'tab', split_axis=1, concat_axis=0, tiled=True)  8.58 us
  transfers between devices with their start and end apart: 8, of which 5 were waited for; matrix products, arithmetic and copies ran while one was open for 7% of the time, Pallas kernels for 0%

profile of v1, /device:TPU:1, one launch (start us, length us, event | category | flops | bytes accessed | tf_op | source)
XLA Modules:
  0.0 344.7 jit_solution(12666276388069028271)
XLA Ops:
  8.0 1.0 select_reduce_fusion
  9.0 0.7 compare_and_fusion
  9.8 0.1 fusion.98
  9.9 1.6 gather_fusion
  11.5 2.4 convolution_convert_fusion
  14.0 3.8 %copy.56 = bf16[2,4096,32]{2,0,1:T(2,128)(2,1)} copy(bf16[2,4096,32]{1,2,0:T(8,128)(2,1)S(1)} %convolution_convert_fusion) | data formatting | bytes 1048576 | tf_op jit(solution)/shard_map/convert_element_type | solution.py:147
  17.8 5.9 %reshape.152 = bf16[32,2,4096]{2,1,0:T(2,128)(2,1)} reshape(bf16[4096,2,32]{2,1,0:T(2,128)(2,1)} %bitcast.166) | data formatting | bytes 1048576
  23.7 8.6 %all-to-all-start = ((bf16[32,2,4096]{2,1,0:T(2,128)(2,1)}), bf16[32,2,4096]{2,1,0:T(2,128)(2,1)S(1)}, u32[]{:S(2)}, u32[]{:S(2)}) async-start(bf16[32,2,4096]{2,1,0:T(2,128)(2,1)} %reshape.152), calls=%async_computation | async-start | bytes 1048576 | tf_op jit(solution)/shard_map/all_to_all | solution.py:148
  32.4 0.8 scatter_custom_fusion
  33.2 0.7 fusion.82
  33.9 10.0 %all-to-all-done = bf16[32,2,4096]{2,1,0:T(2,128)(2,1)S(1)} async-done(((bf16[32,2,4096]{2,1,0:T(2,128)(2,1)}), bf16[32,2,4096]{2,1,0:T(2,128)(2,1)S(1)}, u32[]{:S(2)}, u32[]{:S(2)}) %all-to-all-start) | async-done | bytes 524320 | tf_op jit(solution)/shard_map/all_to_all | solution.py:148
  43.9 2.0 reshape.153
  45.8 4.7 %copy.73 = bf16[2,32,128,32]{2,3,0,1:T(8,128)(2,1)S(1)} copy(bf16[2,32,128,32]{3,0,2,1:T(2,128)(2,1)} %bitcast.167) | data formatting | bytes 1048576 | tf_op jit(solution)/shard_map/all_to_all | solution.py:148
  50.5 0.7 gather_fusion.1
  51.2 0.1 convert_reduce_fusion
  51.4 0.1 convolution_bitcast_fusion.3
  51.5 0.2 fusion.28
  51.7 0.2 convert_reduce_fusion.1
  51.9 0.3 fusion.9
  52.2 0.3 fusion.106
  52.6 0.4 fusion.49
  53.0 0.2 copy-done.5
  53.2 0.5 fusion.19
  53.8 0.2 copy-done.7
  54.0 0.2 copy-done.11
  54.2 0.2 multiply_convert_fusion.1
  54.4 0.8 divide_subtract_fusion
  55.2 0.2 fusion.23
  55.5 1.0 fusion.99
  56.5 3.1 convolution_convert_fusion.1
  59.6 2.0 convolution_bitcast_fusion
  61.7 0.6 broadcast_in_dim.45
  62.3 3.6 %all-to-all-start.1 = ((f32[32,1,128]{2,1,0:T(1,128)}), f32[32,1,128]{2,1,0:T(1,128)S(1)}, u32[]{:S(2)}, u32[]{:S(2)}) async-start(f32[32,1,128]{2,1,0:T(1,128)} %broadcast_in_dim.45), calls=%async_computation.1 | async-start | bytes 32768 | tf_op jit(solution)/shard_map/all_to_all | solution.py:9
  65.9 2.9 fusion.66
  68.9 0.3 copy-done.6
  69.1 0.6 fusion.41
  69.7 0.1 fusion.33
  69.8 0.2 fusion.24
  70.0 0.1 fusion.79
  70.2 0.5 fusion.14
  70.7 0.1 fusion.111
  70.8 1.4 gather_fusion.3
  72.3 0.5 all-to-all-done.1
  72.8 6.8 %all-to-all-start.2 = ((bf16[64,128,32]{1,2,0:T(8,128)(2,1)}), bf16[64,128,32]{1,2,0:T(8,128)(2,1)S(1)}, u32[]{:S(2)}, u32[]{:S(2)}) async-start(bf16[64,128,32]{1,2,0:T(8,128)(2,1)} %gather_fusion.3), calls=%async_computation.2 | async-start | bytes 1048576 | tf_op jit(solution)/shard_map/all_to_all | solution.py:153
  79.7 0.1 fusion.68
  79.8 1.7 convolution_bitcast_fusion.1
  81.5 0.2 copy-done.2
  81.6 0.4 fusion.34
  82.0 15.8 %all-reduce.1 = (f32[64,32]{0,1:T(8,128)S(1)}, f32[32,64]{1,0:T(8,128)S(1)}, f32[32,32]{1,0:T(8,128)S(1)}, f32[256]{0:T(256)S(1)}) all-reduce(f32[64,32]{0,1:T(8,128)S(1)} %fusion.68, f32[32,64]{1,0:T(8,128)S(1)} %fusion.79, f32[32,32]{1,0:T(8,128)S(1)} %fusion.34, f32[256]{0:T(256)S(1)} %bitcast.171), channel_id=1, replica_groups=mesh['tab'=32,'rep'=4] {'rep'}, use_global_device_ids=true, to_apply=%region_9.10 | all-reduce | flops 5376 | bytes 43008 | tf_op jit(solution)/shard_map/psum | solution.py:120
  97.9 123.2 %all-reduce = (f32[64,32]{0,1:T(8,128)}, f32[32,64]{1,0:T(8,128)}, f32[32,32]{1,0:T(8,128)}, f32[256]{0:T(256)}) all-reduce(f32[64,32]{0,1:T(8,128)S(1)} %get-tuple-element.17, f32[32,64]{1,0:T(8,128)S(1)} %get-tuple-element.18, f32[32,32]{1,0:T(8,128)S(1)} %get-tuple-element.19, ...), channel_id=1, replica_groups=mesh['tab'=32,'rep'=4] {'tab'}, use_global_device_ids=true, to_apply=%region_10.11 | all-reduce | flops 5376 | bytes 43008 | tf_op jit(solution)/shard_map/psum | solution.py:120
  221.1 1.1 gather_fusion.2
  222.3 2.1 fusion.29
  224.4 0.6 broadcast_in_dim.49
  225.1 3.3 all-to-all-start.3
  228.4 1.2 and_select_fusion
  229.6 3.2 all-to-all-done.3
  232.8 1.6 broadcast_in_dim.82
  234.4 3.4 all-to-all-start.4
  237.8 2.3 fusion
  240.0 0.6 convert_reduce_fusion.3
  240.6 2.6 all-to-all-done.4
  243.3 0.7 convert_reduce_fusion.2
  243.9 91.6 %all-reduce.7.cloned.1.call-done = f32[256,256]{1,0:T(8,128)} async-done(((f32[256,256]{1,0:T(8,128)}), f32[256,256]{1,0:T(8,128)}) %all-reduce.7.cloned.1.call-update) | async-done | bytes 262160 | tf_op jit(solution)/shard_map/psum | solution.py:120
  335.6 1.7 copy.93
  (42 shorter events, 0.4 us)
Async XLA Ops:
  8.0 45.2 %copy-start = (bf16[4096,256]{1,0:T(8,128)(2,1)S(1)}, bf16[4096,256]{1,0:T(8,128)(2,1)}, u32[]{:S(2)}) copy-start(bf16[4096,256]{1,0:T(8,128)(2,1)} %param.21) | copy-start | bytes 6291460
  17.8 14.5 %copy-start.10 = (s32[64]{0:T(128)S(1)}, s32[64]{0:T(128)}, u32[]{:S(2)}) copy-start(s32[64]{0:T(128)} %param.14) | copy-start | bytes 772
  17.8 14.5 %copy-start.13 = (bf16[256]{0:T(256)(128)(2,1)S(1)}, bf16[256]{0:T(256)(128)(2,1)}, u32[]{:S(2)}) copy-start(bf16[256]{0:T(256)(128)(2,1)} %param.23) | copy-start | bytes 1540
  23.7 20.2 %all-to-all-start = ((bf16[32,2,4096]{2,1,0:T(2,128)(2,1)}), bf16[32,2,4096]{2,1,0:T(2,128)(2,1)S(1)}, u32[]{:S(2)}, u32[]{:S(2)}) async-start(bf16[32,2,4096]{2,1,0:T(2,128)(2,1)} %reshape.152), calls=%async_computation | async-start | bytes 1048576 | tf_op jit(solution)/shard_map/all_to_all | solution.py:148
  32.3 197.3 %all-reduce.5.cloned.1.call-start = ((), (), s32[]{:S(2)}) async-start(), calls=%async_computation.7 | async-start | bytes 524288 | tf_op jit(solution)/shard_map/psum | solution.py:120
  50.5 0.8 copy-start.9
  50.5 1.0 copy-start.12
  50.5 1.3 copy-start.8
  52.2 1.0 copy-start.5
  52.6 1.2 copy-start.3
  53.2 0.8 copy-start.7
  53.2 1.0 copy-start.11
  56.5 176.3 %reduce-scatter.2.cloned.1.call-start = ((), (), s32[]{:S(2)}) async-start(), calls=%async_computation.6 | async-start | bytes 2162688 | tf_op jit(solution)/shard_map/reduce_scatter | solution.py:158
  62.3 10.5 %all-to-all-start.1 = ((f32[32,1,128]{2,1,0:T(1,128)}), f32[32,1,128]{2,1,0:T(1,128)S(1)}, u32[]{:S(2)}, u32[]{:S(2)}) async-start(f32[32,1,128]{2,1,0:T(1,128)} %broadcast_in_dim.45), calls=%async_computation.1 | async-start | bytes 32768 | tf_op jit(solution)/shard_map/all_to_all | solution.py:9
  65.9 2.9 copy-start.1
  65.9 3.2 copy-start.6
  68.8 1.4 copy-start.4
  72.8 149.4 %all-to-all-start.2 = ((bf16[64,128,32]{1,2,0:T(8,128)(2,1)}), bf16[64,128,32]{1,2,0:T(8,128)(2,1)S(1)}, u32[]{:S(2)}, u32[]{:S(2)}) async-start(bf16[64,128,32]{1,2,0:T(8,128)(2,1)} %gather_fusion.3), calls=%async_computation.2 | async-start | bytes 1048576 | tf_op jit(solution)/shard_map/all_to_all | solution.py:153
  79.7 2.0 copy-start.2
  225.1 7.7 %all-to-all-start.3 = ((bf16[4,2,128,32]{2,3,1,0:T(8,128)(2,1)}), bf16[4,2,128,32]{2,3,1,0:T(8,128)(2,1)S(1)}, u32[]{:S(2)}, u32[]{:S(2)}) async-start(bf16[4,2,128,32]{2,3,1,0:T(8,128)(2,1)} %broadcast_in_dim.49), calls=%async_computation.3 | async-start | bytes 131072 | tf_op jit(solution)/shard_map/all_to_all | solution.py:9
  228.3 107.2 %all-reduce.7.cloned.1.call-start = ((), (), s32[]{:S(2)}) async-start(), calls=%async_computation.8 | async-start | bytes 524288 | tf_op jit(solution)/shard_map/psum | solution.py:120
  234.4 8.9 %all-to-all-start.4 = ((bf16[4,128,256]{2,1,0:T(8,128)(2,1)}), bf16[4,128,256]{2,1,0:T(8,128)(2,1)S(1)}, u32[]{:S(2)}, u32[]{:S(2)}) async-start(bf16[4,128,256]{2,1,0:T(8,128)(2,1)} %broadcast_in_dim.82), calls=%async_computation.5 | async-start | bytes 524288 | tf_op jit(solution)/shard_map/all_to_all | solution.py:9
Sparse Core Ops, SparseCore 0:
  56.6 38.5 all-reduce.4
Sparse Core Ops, SparseCore 1:
  60.5 75.2 reduce-scatter.1
  232.1 103.5 all-reduce.6
